TPU v7x, 32 devices: a whole 2x2x4 slice. The times are simulated.
32 devices in a mesh: seq: 4 (over y, x), dp: 8 (over z, core).
Axes of the slice: x: 2, y: 2, z: 4, core: 2. Of those that a mesh axis runs over, the one named last changes fastest.
Arguments:
- tokens: bfloat16 [8, 2048, 768], P('dp', 'seq'), may hold values from -6 to 6
- doc_start: int32 [8, 2048], P('dp'), may hold values from 0 to 2047, as said below
- cotangent: bfloat16 [8, 2048, 768], P('dp', 'seq'), may hold values from -6 to 6
- norm_one: float32 [768], replicated, may hold values from 0.5 to 1.5
- w_qkv: bfloat16 [768, 2304], replicated, may hold values from -0.21875 to 0.21875
- w_out: bfloat16 [768, 768], replicated, may hold values from -0.875 to 0.875
- norm_two: float32 [768], replicated, may hold values from 0.5 to 1.5
- w_in: bfloat16 [768, 2304], replicated, may hold values from -0.21875 to 0.21875
- w_down: bfloat16 [1152, 768], replicated, may hold values from -0.1875 to 0.1875
Outputs:
- result: bfloat16 [8, 2048, 768], P('dp', 'seq')
- grad_tokens: float32 [8, 2048, 768], P('dp', 'seq')
- grad_norm_one: float32 [768], replicated
- grad_w_qkv: float32 [768, 2304], replicated
- grad_w_out: float32 [768, 768], replicated
- grad_norm_two: float32 [768], replicated
- grad_w_in: float32 [768, 2304], replicated
- grad_w_down: float32 [1152, 768], replicated
Inputs may be any that keep to these rules, and one draw needn't show every extreme that they name: Documents are contiguous: doc_start of a token is the place of the first token of its run of equal values, which begins at a place equal to that value; every row begins a document at 0 and ends with a document of one token at place 2048 - 1, and in every row one document starts before 2048 / 8 and runs to place 7 * 256 - 1 or further.
All inputs are finite; a program needn't handle non-finite values.
Results may differ from a plain program's by a relative error of at most 0.013.
Values may be sent and summed in bfloat16 or wider, within the bound.
No kernel may reach another device: no remote copies, remote signals or barrier semaphores. Data moves between devices by JAX's collectives and lax.ppermute only.
A program may use at most 128 MiB of HBM per device.

v0:
```python
import jax
import jax.numpy as jnp
from jax import lax
from jax.sharding import PartitionSpec as P

D = 768
HEADS = 12
HEAD_DIM = 64
FF = 1152
EPSILON = 1e-05
ROTARY_BASE = 160000.0
SCORE_SCALE = 0.125
MASKED_SCORE = -1e30


def layer_norm(values, gain_vec):
    average = jnp.mean(values, axis=-1, keepdims=True)
    centered = values - average
    variance = jnp.mean(centered * centered, axis=-1, keepdims=True)
    return centered * lax.rsqrt(variance + EPSILON) * gain_vec


def rotary_tables(offset):
    half_dim = HEAD_DIM // 2
    frequency = ROTARY_BASE ** (-(jnp.arange(half_dim, dtype=jnp.float32) * 2.0 / HEAD_DIM))
    angles = offset[:, None] * frequency[None, :]
    return (jnp.cos(angles)[:, None, :], jnp.sin(angles)[:, None, :])


def rotate(values, cosine, sine_table):
    half_dim = values.shape[-1] // 2
    first_half = values[..., :half_dim]
    second_half = values[..., half_dim:]
    return jnp.concatenate(
        [
            first_half * cosine - second_half * sine_table,
            second_half * cosine + first_half * sine_table,
        ],
        axis=-1,
    )


def unrotate_three(grad_wide, cosine, sine_table):
    negative_sine = -sine_table
    return jnp.stack(
        [
            rotate(grad_wide[:, 0], cosine, negative_sine),
            rotate(grad_wide[:, 1], cosine, negative_sine),
            grad_wide[:, 2],
        ],
        axis=1,
    )


def gelu_gate(gate_part, up_part):
    return jax.nn.gelu(gate_part, approximate=False) * up_part


def block_scores(query_block, key_heads, block_ids, starts):
    scores = (
        jnp.einsum("qhd,khd->hqk", query_block, key_heads, preferred_element_type=jnp.float32)
        * SCORE_SCALE
    )
    allowed = block_ids[:, None] == starts[None, :]
    return jnp.where(allowed[None], scores, MASKED_SCORE)


def attend_forward(queries, key_heads, value_heads, starts, block_rows):
    row_total = queries.shape[0]

    def attend_block(block_index):
        row_begin = block_index * block_rows
        query_block = lax.dynamic_slice_in_dim(queries, row_begin, block_rows)
        block_ids = lax.dynamic_slice_in_dim(starts, row_begin, block_rows)
        scores = block_scores(query_block, key_heads, block_ids, starts)
        row_max = jnp.max(scores, axis=-1, keepdims=True)
        weight = jnp.exp(scores - row_max)
        row_sum = jnp.sum(weight, axis=-1, keepdims=True)
        probs = (weight / row_sum).astype(jnp.bfloat16)
        context = jnp.einsum("hqk,khd->qhd", probs, value_heads, preferred_element_type=jnp.float32)
        return (context, row_max, row_sum)

    context, row_max, row_sum = lax.map(
        attend_block, jnp.arange(row_total // block_rows, dtype=jnp.int32)
    )
    return (context.reshape(queries.shape), row_max, row_sum)


def attend_backward(
    queries, key_heads, value_heads, grad_context, starts, row_max, row_sum, block_rows
):
    row_total = queries.shape[0]

    def back_block(carry, block_index):
        grad_key, grad_value = carry
        row_begin = block_index * block_rows
        query_block = lax.dynamic_slice_in_dim(queries, row_begin, block_rows)
        grad_block = lax.dynamic_slice_in_dim(grad_context, row_begin, block_rows)
        block_ids = lax.dynamic_slice_in_dim(starts, row_begin, block_rows)
        scores = block_scores(query_block, key_heads, block_ids, starts)
        probs = jnp.exp(scores - row_max[block_index]) / row_sum[block_index]
        probs_low = probs.astype(jnp.bfloat16)
        grad_value = grad_value + jnp.einsum(
            "hqk,qhd->khd", probs_low, grad_block, preferred_element_type=jnp.float32
        )
        grad_prob = jnp.einsum(
            "qhd,khd->hqk", grad_block, value_heads, preferred_element_type=jnp.float32
        )
        centre = jnp.sum(grad_prob * probs, axis=-1, keepdims=True)
        grad_scores = (probs * (grad_prob - centre)).astype(jnp.bfloat16)
        grad_query = (
            jnp.einsum("hqk,khd->qhd", grad_scores, key_heads, preferred_element_type=jnp.float32)
            * SCORE_SCALE
        )
        grad_key = (
            grad_key
            + jnp.einsum(
                "hqk,qhd->khd", grad_scores, query_block, preferred_element_type=jnp.float32
            )
            * SCORE_SCALE
        )
        return ((grad_key, grad_value), grad_query)

    zero_heads = jnp.zeros(queries.shape, jnp.float32)
    (grad_key, grad_value), grad_query = lax.scan(
        back_block, (zero_heads, zero_heads), jnp.arange(row_total // block_rows, dtype=jnp.int32)
    )
    return (grad_query.reshape(queries.shape), grad_key, grad_value)


def on_device(tokens, doc_start, cotangent, norm_one, w_qkv, w_out, norm_two, w_in, w_down):
    seq_parts = lax.axis_size("seq")
    shard_len = tokens.shape[1]
    row_total = shard_len * seq_parts
    head_width = D // seq_parts
    group_heads = HEADS // seq_parts
    block_rows = min(512, row_total)
    first_token = lax.axis_index("seq") * shard_len
    hidden = tokens[0].astype(jnp.float32)
    starts = doc_start[0]
    own_starts = lax.dynamic_slice_in_dim(starts, first_token, shard_len)
    offset = (first_token + jnp.arange(shard_len, dtype=jnp.int32) - own_starts).astype(jnp.float32)
    cosine, sine_table = rotary_tables(offset)
    normed_one, norm_one_back = jax.vjp(layer_norm, hidden, norm_one)
    normed_one_low = normed_one.astype(jnp.bfloat16)
    projected = jnp.dot(normed_one_low, w_qkv, preferred_element_type=jnp.float32).reshape(
        shard_len, 3, HEADS, HEAD_DIM
    )
    turned = jnp.stack(
        [
            rotate(projected[:, 0], cosine, sine_table),
            rotate(projected[:, 1], cosine, sine_table),
            projected[:, 2],
        ],
        axis=1,
    ).astype(jnp.bfloat16)
    outgoing = turned.reshape(shard_len, 3, seq_parts, head_width)
    incoming = lax.all_to_all(outgoing, "seq", split_axis=2, concat_axis=0, tiled=True)
    queries = incoming[:, 0, 0].reshape(row_total, group_heads, HEAD_DIM)
    key_heads = incoming[:, 1, 0].reshape(row_total, group_heads, HEAD_DIM)
    value_heads = incoming[:, 2, 0].reshape(row_total, group_heads, HEAD_DIM)
    context, row_max, row_sum = attend_forward(queries, key_heads, value_heads, starts, block_rows)
    context_send = context.astype(jnp.bfloat16).reshape(row_total, 1, head_width)
    context_tok = lax.all_to_all(
        context_send, "seq", split_axis=0, concat_axis=1, tiled=True
    ).reshape(shard_len, D)
    attended = jnp.dot(context_tok, w_out, preferred_element_type=jnp.float32)
    middle = hidden + attended
    normed_two, norm_two_back = jax.vjp(layer_norm, middle, norm_two)
    normed_two_low = normed_two.astype(jnp.bfloat16)
    gate_up = jnp.dot(normed_two_low, w_in, preferred_element_type=jnp.float32)
    inner, gelu_back = jax.vjp(gelu_gate, gate_up[:, :FF], gate_up[:, FF:])
    inner_low = inner.astype(jnp.bfloat16)
    result = (middle + jnp.dot(inner_low, w_down, preferred_element_type=jnp.float32)).astype(
        jnp.bfloat16
    )
    grad_out = cotangent[0]
    grad_w_down = jnp.einsum("tf,td->fd", inner_low, grad_out, preferred_element_type=jnp.float32)
    grad_inner = jnp.einsum("td,fd->tf", grad_out, w_down, preferred_element_type=jnp.float32)
    grad_gate, grad_up = gelu_back(grad_inner)
    grad_gate_up = jnp.concatenate([grad_gate, grad_up], axis=-1).astype(jnp.bfloat16)
    grad_w_in = jnp.einsum(
        "td,tf->df", normed_two_low, grad_gate_up, preferred_element_type=jnp.float32
    )
    grad_normed_two = jnp.einsum(
        "tf,df->td", grad_gate_up, w_in, preferred_element_type=jnp.float32
    )
    grad_middle_part, grad_norm_two = norm_two_back(grad_normed_two)
    grad_middle = grad_out.astype(jnp.float32) + grad_middle_part
    grad_mid_low = grad_middle.astype(jnp.bfloat16)
    grad_w_out = jnp.einsum(
        "td,te->de", context_tok, grad_mid_low, preferred_element_type=jnp.float32
    )
    grad_context_tok = jnp.einsum(
        "te,de->td", grad_mid_low, w_out, preferred_element_type=jnp.float32
    ).astype(jnp.bfloat16)
    grad_context = lax.all_to_all(
        grad_context_tok.reshape(shard_len, seq_parts, head_width),
        "seq",
        split_axis=1,
        concat_axis=0,
        tiled=True,
    )
    grad_context = grad_context.reshape(row_total, group_heads, HEAD_DIM)
    grad_query, grad_key, grad_value = attend_backward(
        queries, key_heads, value_heads, grad_context, starts, row_max, row_sum, block_rows
    )
    grad_heads = jnp.stack([grad_query, grad_key, grad_value], axis=1).astype(jnp.bfloat16)
    grad_tok = lax.all_to_all(
        grad_heads.reshape(row_total, 3, 1, head_width),
        "seq",
        split_axis=0,
        concat_axis=2,
        tiled=True,
    )
    grad_tok = grad_tok.reshape(shard_len, 3, HEADS, HEAD_DIM)
    grad_projected = unrotate_three(grad_tok.astype(jnp.float32), cosine, sine_table)
    grad_projected = grad_projected.astype(jnp.bfloat16).reshape(shard_len, 3 * D)
    grad_normed_one = jnp.einsum(
        "tf,df->td", grad_projected, w_qkv, preferred_element_type=jnp.float32
    )
    grad_hidden_part, grad_norm_one = norm_one_back(grad_normed_one)
    grad_input = grad_middle + grad_hidden_part
    grad_w_qkv = jnp.einsum(
        "td,tf->df", normed_one_low, grad_projected, preferred_element_type=jnp.float32
    )
    summed = lax.psum(
        (grad_norm_one, grad_w_qkv, grad_w_out, grad_norm_two, grad_w_in, grad_w_down),
        ("seq", "dp"),
    )
    return (
        result[None],
        grad_input[None],
        summed[0],
        summed[1],
        summed[2],
        summed[3],
        summed[4],
        summed[5],
    )


def solution(mesh):
    placed = (
        P("dp", "seq", None),
        P("dp", None),
        P("dp", "seq", None),
        P(),
        P(),
        P(),
        P(),
        P(),
        P(),
    )
    return jax.shard_map(
        on_device,
        mesh=mesh,
        in_specs=placed,
        out_specs=(P("dp", "seq", None), P("dp", "seq", None), P(), P(), P(), P(), P(), P()),
        check_vma=False,
    )
```

profile of v0, /device:TPU:0, one launch (start us, length us, event | category | flops | bytes accessed | tf_op | source)
XLA Modules:
  0.0 809.1 jit_solution(15965780885867940108)
XLA Ops:
  7.2 5.9 copy.68
  16.5 4.5 fusion.55
  30.1 5.4 all-to-all-start
  35.5 28.5 %all-to-all-done = bf16[512,3,4,192]{0,3,1,2:T(8,128)(2,1)} async-done(((bf16[512,3,4,192]{0,3,1,2:T(8,128)(2,1)}), bf16[512,3,4,192]{0,3,1,2:T(8,128)(2,1)}, u32[]{:S(2)}, u32[]{:S(2)}) %all-to-all-start) | async-done | bytes 2359328 | tf_op jit(solution)/shard_map/all_to_all | solution.py:158
  68.4 99.3 %while.29 = (s32[]{:T(128)}, bf16[4,512,3,64]{1,3,2,0:T(8,128)(2,1)}, f32[4,3,512,1]{2,1,3,0:T(4,128)}, f32[4,3,512,1]{2,1,3,0:T(4,128)}, s32[4]{0:T(128)S(1)}, ...) while((s32[]{:T(128)}, ...), condition=%wide.region_5.6_spmd, body=%wide.region_2.5_spmd.sunk | while | flops 844100608 | bytes 53621036 | solution.py:83
  70.4 8.3 %fusion.119 = (f32[3,512]{1,0:T(4,128)S(1)}, f32[3,512,2048]{2,1,0:T(8,128)}) fusion(pred[512,2048]{1,0:T(8,128)(4,1)S(1)} %broadcast_compare_fusion.4, bf16[2048,3,64]{0,2,1:T(8,128)(2,1)} %get-tuple-element.471, bf16[2048,3,64]{0,2,1:T(8,128)(2,1)} %get-tuple-element.470, s32[]{:T(128)S(6)} %select_n.52), kind=kOutput, calls=%fused_computation.3.clone.1 | convolution fusion | flops 412088832 | bytes 14620676 | tf_op jit(solution)/shard_map/while/body/eval_jaxpr/qhd,khd->hqk/dot_general | solution.py:61
  78.7 6.9 fusion.120
  85.6 6.8 fusion.121
  95.2 8.3 %fusion.119 = (f32[3,512]{1,0:T(4,128)S(1)}, f32[3,512,2048]{2,1,0:T(8,128)}) fusion(pred[512,2048]{1,0:T(8,128)(4,1)S(1)} %broadcast_compare_fusion.4, bf16[2048,3,64]{0,2,1:T(8,128)(2,1)} %get-tuple-element.471, bf16[2048,3,64]{0,2,1:T(8,128)(2,1)} %get-tuple-element.470, s32[]{:T(128)S(6)} %select_n.52), kind=kOutput, calls=%fused_computation.3.clone.1 | convolution fusion | flops 412088832 | bytes 14620676 | tf_op jit(solution)/shard_map/while/body/eval_jaxpr/qhd,khd->hqk/dot_general | solution.py:61
  103.5 6.9 fusion.120
  110.4 6.8 fusion.121
  120.0 8.3 %fusion.119 = (f32[3,512]{1,0:T(4,128)S(1)}, f32[3,512,2048]{2,1,0:T(8,128)}) fusion(pred[512,2048]{1,0:T(8,128)(4,1)S(1)} %broadcast_compare_fusion.4, bf16[2048,3,64]{0,2,1:T(8,128)(2,1)} %get-tuple-element.471, bf16[2048,3,64]{0,2,1:T(8,128)(2,1)} %get-tuple-element.470, s32[]{:T(128)S(6)} %select_n.52), kind=kOutput, calls=%fused_computation.3.clone.1 | convolution fusion | flops 412088832 | bytes 14620676 | tf_op jit(solution)/shard_map/while/body/eval_jaxpr/qhd,khd->hqk/dot_general | solution.py:61
  128.3 6.9 fusion.120
  135.2 6.8 fusion.121
  144.9 8.3 %fusion.119 = (f32[3,512]{1,0:T(4,128)S(1)}, f32[3,512,2048]{2,1,0:T(8,128)}) fusion(pred[512,2048]{1,0:T(8,128)(4,1)S(1)} %broadcast_compare_fusion.4, bf16[2048,3,64]{0,2,1:T(8,128)(2,1)} %get-tuple-element.471, bf16[2048,3,64]{0,2,1:T(8,128)(2,1)} %get-tuple-element.470, s32[]{:T(128)S(6)} %select_n.52), kind=kOutput, calls=%fused_computation.3.clone.1 | convolution fusion | flops 412088832 | bytes 14620676 | tf_op jit(solution)/shard_map/while/body/eval_jaxpr/qhd,khd->hqk/dot_general | solution.py:61
  153.2 6.9 fusion.120
  160.0 6.8 fusion.121
  170.3 2.8 convert_element_type.105
  173.6 3.0 reduce.1
  178.9 3.9 reshape.373
  182.8 15.3 %all_to_all.57 = bf16[4,2,49152]{2,1,0:T(2,128)(2,1)} all-to-all(bf16[4,2,49152]{2,1,0:T(2,128)(2,1)} %reshape.373), channel_id=1, replica_groups=mesh['seq'=4,'dp'=8] {'seq'}, dimensions={0} | all-to-all | bytes 1572864 | tf_op jit(solution)/shard_map/all_to_all | solution.py:164
  198.1 4.1 reshape.374
  202.2 5.7 copy.75
  208.0 3.4 all_to_all.47
  217.9 6.1 add_convert_fusion
  233.1 4.2 all-to-all-start.2
  237.3 9.3 %all-to-all-done.2 = bf16[512,4,192]{0,2,1:T(8,128)(2,1)} async-done(((bf16[512,4,192]{0,2,1:T(8,128)(2,1)}), bf16[512,4,192]{0,2,1:T(8,128)(2,1)}, u32[]{:S(2)}, u32[]{:S(2)}) %all-to-all-start.2) | async-done | bytes 786464 | tf_op jit(solution)/shard_map/all_to_all | solution.py:197
  249.2 2.8 reshape.369
  252.9 125.6 %while.30 = (s32[]{:T(128)}, f32[2048,3,64]{0,2,1:T(8,128)S(1)}, f32[2048,3,64]{0,2,1:T(8,128)S(1)}, bf16[4,512,3,64]{1,3,2,0:T(8,128)(2,1)}, s32[4]{0:T(128)S(1...) while((s32[]{:T(128)}, f32[2048,3,64]{0,2,1:T(8,128)S(1)}, ...), condition=%wide.region_12.13_spmd.clone, body=%wide.region_10.12_spmd.clone.sunk | while | flops 2047834624 | bytes 185006560 | solution.py:125
  257.6 5.0 exponential_divide_fusion.2
  262.6 4.1 multiply_reduce_fusion.5
  267.2 3.5 multiply_convert_fusion.7
  270.7 4.4 fusion.131
  275.1 6.2 fusion.132
  289.0 5.0 exponential_divide_fusion.2
  294.0 4.1 multiply_reduce_fusion.5
  298.5 3.5 multiply_convert_fusion.7
  302.0 4.4 fusion.131
  306.5 6.2 fusion.132
  320.3 5.0 exponential_divide_fusion.2
  325.3 4.1 multiply_reduce_fusion.5
  329.9 3.5 multiply_convert_fusion.7
  333.4 4.4 fusion.131
  337.8 6.2 fusion.132
  351.7 5.0 exponential_divide_fusion.2
  356.7 4.1 multiply_reduce_fusion.5
  361.3 3.5 multiply_convert_fusion.7
  364.7 4.4 fusion.131
  369.2 6.2 fusion.132
  383.4 4.7 copy.80
  388.1 5.0 all-to-all-start.3
  395.4 2.9 fusion.57
  398.4 5.1 fusion.51
  403.5 35.6 %all-to-all-done.3 = bf16[2048,3,1,192]{3,1,2,0:T(4,128)(2,1)} async-done(((bf16[2048,3,1,192]{3,1,2,0:T(4,128)(2,1)}), bf16[2048,3,1,192]{3,1,2,0:T(4,128)(2,1)}, u32[]{:S(2)}, u32[]{:S(2)}) %all-to-all-start.3) | async-done | bytes 2359328 | tf_op jit(solution)/shard_map/all_to_all | solution.py:209
  439.1 6.9 copy.81
  446.0 6.4 reshape.371
  452.5 3.9 copy.82
  459.7 5.3 fusion.61
  465.1 4.0 fusion.53
  473.3 40.5 %all-reduce = (f32[768]{0:T(1024)}, f32[768]{0:T(1024)}) all-reduce(f32[768]{0:T(1024)S(1)} %get-tuple-element.181, f32[768]{0:T(1024)S(1)} %copy-done.54), channel_id=1, replica_groups=mesh['seq'=4,'dp'=8] {'seq','dp'}, use_global_device_ids=true, to_apply=%region_16.17 | all-reduce | flops 1536 | bytes 12288 | tf_op jit(solution)/shard_map/psum | solution.py:227
  513.8 3.3 add_bitcast_fusion
  517.0 269.9 %all-reduce.4.cloned.1.call-done = (f32[768,2304]{1,0:T(8,128)}, f32[768,768]{1,0:T(8,128)}, f32[768,2304]{1,0:T(8,128)}, f32[1152,768]{1,0:T(8,128)}) async-done(((f32[768,2304]{1,0:T(8,128)}, f32[768,768]{1,0:T(8,128)}, f32[768,2304]{1,0:T(8,128)}, f32[1152,768]{1,0:T(8,128)}), (f32[768,2304]{1,0:T(8,128)}, f32[768,768]{1,0:T(8,128)}, f32[768,2304]{1,0:T(8,128)}, ...) | async-done | bytes 20054032 | tf_op jit(solution)/shard_map/psum | solution.py:227
  786.9 7.2 copy.118
  795.5 3.6 copy.120
  (273 shorter events, 90.1 us)
Async XLA Ops:
  7.2 208.6 %copy-start = (bf16[768,2304]{1,0:T(8,128)(2,1)S(1)}, bf16[768,2304]{1,0:T(8,128)(2,1)}, u32[]{:S(2)}) copy-start(bf16[768,2304]{1,0:T(8,128)(2,1)} %param.20) | copy-start | bytes 10616836
  7.2 9.3 %copy-start.52 = (f32[768]{0:T(1024)S(1)}, f32[768]{0:T(1024)}, u32[]{:S(2)}) copy-start(f32[768]{0:T(1024)} %param.16) | copy-start | bytes 9220
  14.4 6.5 copy-start.44
  16.5 4.5 copy-start.46
  24.9 2.4 copy-start.35
  30.1 34.0 %all-to-all-start = ((bf16[512,3,4,192]{0,3,1,2:T(8,128)(2,1)}), bf16[512,3,4,192]{0,3,1,2:T(8,128)(2,1)}, u32[]{:S(2)}, u32[]{:S(2)}) async-start(bf16[512,3,4,192]{0,3,1,2:T(8,128)(2,1)} %pad_maximum_fusion), calls=%async_computation | async-start | bytes 4718592 | tf_op jit(solution)/shard_map/all_to_all | solution.py:158
  78.7 6.9 copy-start.3
  78.7 6.9 copy-start.23
  103.5 6.9 copy-start.3
  103.5 6.9 copy-start.23
  128.3 6.9 copy-start.3
  128.3 6.9 copy-start.23
  153.1 6.9 copy-start.3
  153.2 6.9 copy-start.23
  212.7 3.0 copy-start.25
  212.7 3.1 copy-start.38
  215.4 13.2 %copy-start.5 = (f32[512,768]{1,0:T(8,128)}, f32[512,768]{1,0:T(8,128)S(1)}, u32[]{:S(2)}) copy-start(f32[512,768]{1,0:T(8,128)S(1)} %get-tuple-element.272) | copy-start | bytes 4718596
  215.4 13.2 %copy-start.40 = (f32[512]{0:T(512)}, f32[512]{0:T(512)S(1)}, u32[]{:S(2)}) copy-start(f32[512]{0:T(512)S(1)} %broadcast_multiply_fusion) | copy-start | bytes 6148
  215.7 12.8 %copy-start.42 = (f32[512]{0:T(512)}, f32[512]{0:T(512)S(1)}, u32[]{:S(2)}) copy-start(f32[512]{0:T(512)S(1)} %fusion.65) | copy-start | bytes 6148
  215.8 2.1 copy-start.11
  225.7 2.8 copy-start.15
  229.2 2.7 copy-start.7
  233.1 13.5 %all-to-all-start.2 = ((bf16[512,4,192]{0,2,1:T(8,128)(2,1)}), bf16[512,4,192]{0,2,1:T(8,128)(2,1)}, u32[]{:S(2)}, u32[]{:S(2)}) async-start(bf16[512,4,192]{0,2,1:T(8,128)(2,1)} %bitcast.31), calls=%async_computation.2 | async-start | bytes 1572864 | tf_op jit(solution)/shard_map/all_to_all | solution.py:197
  262.6 4.6 copy-start.2
  270.7 10.7 %slice-start = ((s8[6291456]{0:T(1024)(128)(4,1)}), s8[4194304]{0:T(1024)(128)(4,1)S(1)}, s32[]{:S(2)}) async-start(s8[6291456]{0:T(1024)(128)(4,1)} %bitcast.196), calls=%async_computation.5 | async-start | bytes 8388608 | tf_op jit(solution)/shard_map/while
  275.1 6.3 slice-start.1
  275.1 6.3 copy-start.4
  275.1 6.3 copy-start.20
  294.0 4.6 copy-start.2
  302.0 10.7 %slice-start = ((s8[6291456]{0:T(1024)(128)(4,1)}), s8[4194304]{0:T(1024)(128)(4,1)S(1)}, s32[]{:S(2)}) async-start(s8[6291456]{0:T(1024)(128)(4,1)} %bitcast.196), calls=%async_computation.5 | async-start | bytes 8388608 | tf_op jit(solution)/shard_map/while
  306.4 6.3 slice-start.1
  306.4 6.3 copy-start.4
  306.5 6.3 copy-start.20
  325.3 4.6 copy-start.2
  333.4 10.7 %slice-start = ((s8[6291456]{0:T(1024)(128)(4,1)}), s8[4194304]{0:T(1024)(128)(4,1)S(1)}, s32[]{:S(2)}) async-start(s8[6291456]{0:T(1024)(128)(4,1)} %bitcast.196), calls=%async_computation.5 | async-start | bytes 8388608 | tf_op jit(solution)/shard_map/while
  337.8 6.3 slice-start.1
  337.8 6.3 copy-start.4
  337.8 6.3 copy-start.20
  356.7 4.6 copy-start.2
  364.7 10.7 %slice-start = ((s8[6291456]{0:T(1024)(128)(4,1)}), s8[4194304]{0:T(1024)(128)(4,1)S(1)}, s32[]{:S(2)}) async-start(s8[6291456]{0:T(1024)(128)(4,1)} %bitcast.196), calls=%async_computation.5 | async-start | bytes 8388608 | tf_op jit(solution)/shard_map/while
  369.2 6.3 slice-start.1
  369.2 6.3 copy-start.4
  369.2 6.3 copy-start.20
  388.1 5.1 copy-start.26
  388.1 5.1 copy-start.28
  388.1 51.0 %all-to-all-start.3 = ((bf16[2048,3,1,192]{3,1,2,0:T(4,128)(2,1)}), bf16[2048,3,1,192]{3,1,2,0:T(4,128)(2,1)}, u32[]{:S(2)}, u32[]{:S(2)}) async-start(bf16[2048,3,1,192]{3,1,2,0:T(4,128)(2,1)} %copy.80), calls=%async_computation.3 | async-start | bytes 8388608 | tf_op jit(solution)/shard_map/all_to_all | solution.py:209
  393.1 2.2 copy-start.12
  393.1 393.7 %all-reduce.4.cloned.1.call-start = ((), (), s32[]{:S(2)}) async-start(), calls=%async_computation.4 | async-start | bytes 40108032 | tf_op jit(solution)/shard_map/psum | solution.py:227
  393.2 2.2 copy-start.13
  395.4 3.0 copy-start.6
  395.4 3.0 copy-start.16
  395.4 3.0 copy-start.34
  395.4 3.0 copy-start.39
  395.4 2.9 copy-start.41
  395.4 2.9 copy-start.43
  465.0 4.1 copy-start.17
  465.0 4.1 copy-start.31
  469.1 2.3 copy-start.51
  471.4 42.4 %copy-start.8 = (f32[512,768]{1,0:T(8,128)S(1)}, f32[512,768]{1,0:T(8,128)}, u32[]{:S(2)}) copy-start(f32[512,768]{1,0:T(8,128)} %copy-done.7) | copy-start | bytes 4718596
  471.4 42.4 %copy-start.49 = (f32[512]{0:T(512)S(1)}, f32[512]{0:T(512)}, u32[]{:S(2)}) copy-start(f32[512]{0:T(512)} %copy-done.48) | copy-start | bytes 6148
  786.9 7.2 copy-start.29
  786.9 8.6 %copy-start.10 = (f32[768,2304]{1,0:T(8,128)S(1)}, f32[768,2304]{1,0:T(8,128)}, u32[]{:S(2)}) copy-start(f32[768,2304]{1,0:T(8,128)} %get-tuple-element.537) | copy-start | bytes 21233668
  795.5 4.6 copy-start.18
  795.5 6.4 copy-start.1
  (26 other events, 34.0 us)
Sparse Core Ops, SparseCore 0:
  465.2 321.6 all-reduce.3
where the time goes:
time: 816 us; the launch traced here: 809 us
  waiting for transfers between devices  343 us (42%)
  matrix products  188 us (23%)
  local copies, waits for them, and re-layouts  109 us (13%)
  other arithmetic  69.3 us (8%)
  blocking collectives  55.8 us (7%)
  between operations  15.1 us (2%)
  starting transfers between devices  14.6 us (2%)
  loops' own time  13.8 us (2%)
    psum x1, waiting for transfers between devices, on_device(): lax.psum((grad_norm_one, grad_w_qkv, grad_w_out, grad_norm_two, grad_w_in...  270 us
    dot_general x8, matrix products, block_scores(): jnp.einsum('qhd,khd->hqk', query_block, key_heads, preferred_element_type...  53.2 us
    psum x1, blocking collectives, on_device(): lax.psum((grad_norm_one, grad_w_qkv, grad_w_out, grad_norm_two, grad_w_in...  40.5 us
    unnamed x108, local copies, waits for them, and re-layouts  37.3 us
    all_to_all x1, waiting for transfers between devices, on_device(): lax.all_to_all(grad_heads.reshape(row_total, 3, 1, head_width), 'seq', sp...  35.6 us
    all_to_all x1, waiting for transfers between devices, on_device(): lax.all_to_all(outgoing, 'seq', split_axis=2, concat_axis=0, tiled=True)  28.5 us
    reduce_sum x4, other arithmetic, attend_block(): row_sum = jnp.sum(weight, axis=-1, keepdims=True)  27.5 us
    dot_general x4, matrix products, attend_block(): jnp.einsum('hqk,khd->qhd', probs, value_heads, preferred_element_type=jnp...  27 us
  transfers between devices with their start and end apart: 4, of which 4 were waited for; matrix products, arithmetic and copies ran while one was open for 3% of the time, Pallas kernels for 0%

commit v1 on v0

--- a/solution.py
+++ b/solution.py
@@ -225,8 +225,10 @@
         "td,tf->df", normed_one_low, grad_projected, preferred_element_type=jnp.float32
     )
     summed = lax.psum(
-        (grad_norm_one, grad_w_qkv, grad_w_out, grad_norm_two, grad_w_in, grad_w_down),
-        ("seq", "dp"),
+        lax.psum(
+            (grad_norm_one, grad_w_qkv, grad_w_out, grad_norm_two, grad_w_in, grad_w_down), "dp"
+        ),
+        "seq",
     )
     return (
         result[None],

time: 816 us -> 1260 us (1.54)
  waiting for transfers between devices: 343 us -> 798 us
  blocking collectives: 55.8 us -> 42.3 us
    psum x0 -> x1, waiting for transfers between devices: none -> 329 us  [on_device(): lax.psum(lax.psum((grad_norm_one, grad_w_qkv, grad_w_out, grad_norm_two,...]
    psum x1, waiting for transfers between devices: 270 us -> 396 us  [on_device(): lax.psum((grad_norm_one, grad_w_qkv, grad_w_out, grad_norm_two, grad_w_in...]
    psum x1, blocking collectives: 40.5 us -> 16 us  [on_device(): lax.psum((grad_norm_one, grad_w_qkv, grad_w_out, grad_norm_two, grad_w_in...]
  transfers between devices with their start and end apart: 4 -> 5, of which waited for: 4 -> 5; matrix products, arithmetic and copies ran while one was open for 3% -> 2% of each run, Pallas kernels for 0% -> 0%
where the time goes in v1:
time: 1260 us; the launch traced here: 1250 us
  waiting for transfers between devices  798 us (63%)
  matrix products  188 us (15%)
  local copies, waits for them, and re-layouts  109 us (9%)
  other arithmetic  69.2 us (5%)
  blocking collectives  42.3 us (3%)
  between operations  15.2 us (1%)
  starting transfers between devices  14.7 us (1%)
  loops' own time  13.8 us (1%)
    psum x1, waiting for transfers between devices, on_device(): lax.psum((grad_norm_one, grad_w_qkv, grad_w_out, grad_norm_two, grad_w_in...  396 us
    psum x1, waiting for transfers between devices, on_device(): lax.psum(lax.psum((grad_norm_one, grad_w_qkv, grad_w_out, grad_norm_two,...  329 us
    dot_general x8, matrix products, block_scores(): jnp.einsum('qhd,khd->hqk', query_block, key_heads, preferred_element_type...  53.2 us
    unnamed x108, local copies, waits for them, and re-layouts  37.3 us
    all_to_all x1, waiting for transfers between devices, on_device(): lax.all_to_all(grad_heads.reshape(row_total, 3, 1, head_width), 'seq', sp...  35.3 us
    all_to_all x1, waiting for transfers between devices, on_device(): lax.all_to_all(outgoing, 'seq', split_axis=2, concat_axis=0, tiled=True)  28.5 us
    reduce_sum x4, other arithmetic, attend_block(): row_sum = jnp.sum(weight, axis=-1, keepdims=True)  27.5 us
    dot_general x4, matrix products, attend_block(): jnp.einsum('hqk,khd->qhd', probs, value_heads, preferred_element_type=jnp...  27 us
  transfers between devices with their start and end apart: 5, of which 5 were waited for; matrix products, arithmetic and copies ran while one was open for 2% of the time, Pallas kernels for 0%

profile of v1, /device:TPU:0, one launch (start us, length us, event | category | flops | bytes accessed | tf_op | source)
XLA Modules:
  0.0 1250.4 jit_solution(11981540001177254347)
XLA Ops:
  7.2 5.9 copy.68
  16.5 4.5 fusion.55
  30.1 5.4 all-to-all-start
  35.6 28.5 %all-to-all-done = bf16[512,3,4,192]{0,3,1,2:T(8,128)(2,1)} async-done(((bf16[512,3,4,192]{0,3,1,2:T(8,128)(2,1)}), bf16[512,3,4,192]{0,3,1,2:T(8,128)(2,1)}, u32[]{:S(2)}, u32[]{:S(2)}) %all-to-all-start) | async-done | bytes 2359328 | tf_op jit(solution)/shard_map/all_to_all | solution.py:158
  68.5 99.3 %while.29 = (s32[]{:T(128)}, bf16[4,512,3,64]{1,3,2,0:T(8,128)(2,1)}, f32[4,3,512,1]{2,1,3,0:T(4,128)}, f32[4,3,512,1]{2,1,3,0:T(4,128)}, s32[4]{0:T(128)S(1)}, ...) while((s32[]{:T(128)}, ...), condition=%wide.region_5.6_spmd, body=%wide.region_2.5_spmd.sunk | while | flops 844100608 | bytes 53621036 | solution.py:83
  70.4 8.3 fusion.119
  78.7 6.9 fusion.120
  85.6 6.8 fusion.121
  95.3 8.3 fusion.119
  103.6 6.9 fusion.120
  110.5 6.8 fusion.121
  120.1 8.3 fusion.119
  128.4 6.9 fusion.120
  135.3 6.8 fusion.121
  144.9 8.3 fusion.119
  153.2 6.9 fusion.120
  160.1 6.8 fusion.121
  173.7 3.0 reduce.1
  178.9 3.9 reshape.373
  182.8 15.3 %all_to_all.57 = bf16[4,2,49152]{2,1,0:T(2,128)(2,1)} all-to-all(bf16[4,2,49152]{2,1,0:T(2,128)(2,1)} %reshape.373), channel_id=1, replica_groups=mesh['seq'=4,'dp'=8] {'seq'}, dimensions={0} | all-to-all | bytes 1572864 | tf_op jit(solution)/shard_map/all_to_all | solution.py:164
  198.2 4.1 reshape.374
  202.3 5.7 copy.75
  208.0 3.4 all_to_all.47
  218.0 6.1 add_convert_fusion
  233.0 4.2 all-to-all-start.2
  237.2 9.2 all-to-all-done.2
  252.8 125.6 %while.30 = (s32[]{:T(128)}, f32[2048,3,64]{0,2,1:T(8,128)S(1)}, f32[2048,3,64]{0,2,1:T(8,128)S(1)}, bf16[4,512,3,64]{1,3,2,0:T(8,128)(2,1)}, s32[4]{0:T(128)S(1...) while((s32[]{:T(128)}, f32[2048,3,64]{0,2,1:T(8,128)S(1)}, ...), condition=%wide.region_12.13_spmd.clone, body=%wide.region_10.12_spmd.clone.sunk | while | flops 2047834624 | bytes 185006560 | solution.py:125
  257.4 5.0 exponential_divide_fusion.2
  262.4 4.1 multiply_reduce_fusion.5
  267.0 3.5 multiply_convert_fusion.7
  270.5 4.4 fusion.131
  274.9 6.2 fusion.132
  288.8 5.0 exponential_divide_fusion.2
  293.8 4.1 multiply_reduce_fusion.5
  298.3 3.5 multiply_convert_fusion.7
  301.8 4.4 fusion.131
  306.3 6.2 fusion.132
  320.1 5.0 exponential_divide_fusion.2
  325.1 4.1 multiply_reduce_fusion.5
  329.7 3.5 multiply_convert_fusion.7
  333.2 4.4 fusion.131
  337.6 6.2 fusion.132
  351.5 5.0 exponential_divide_fusion.2
  356.5 4.1 multiply_reduce_fusion.5
  361.1 3.5 multiply_convert_fusion.7
  364.6 4.4 fusion.131
  369.0 6.2 fusion.132
  383.2 4.7 copy.80
  387.9 5.0 all-to-all-start.3
  395.2 2.9 fusion.57
  398.2 5.1 fusion.51
  403.3 35.3 %all-to-all-done.3 = bf16[2048,3,1,192]{3,1,2,0:T(4,128)(2,1)} async-done(((bf16[2048,3,1,192]{3,1,2,0:T(4,128)(2,1)}), bf16[2048,3,1,192]{3,1,2,0:T(4,128)(2,1)}, u32[]{:S(2)}, u32[]{:S(2)}) %all-to-all-start.3) | async-done | bytes 2359328 | tf_op jit(solution)/shard_map/all_to_all | solution.py:209
  438.6 6.9 copy.81
  445.5 6.4 reshape.371
  452.0 3.9 copy.82
  459.2 5.3 fusion.61
  464.6 396.2 %all-reduce.7.cloned.1.call-done = (f32[768,2304]{1,0:T(8,128)}, f32[768,768]{1,0:T(8,128)}, f32[768,2304]{1,0:T(8,128)}, f32[1152,768]{1,0:T(8,128)}) async-done(((f32[768,2304]{1,0:T(8,128)}, f32[768,768]{1,0:T(8,128)}, f32[768,2304]{1,0:T(8,128)}, f32[1152,768]{1,0:T(8,128)}), (f32[768,2304]{1,0:T(8,128)}, f32[768,768]{1,0:T(8,128)}, f32[768,2304]{1,0:T(8,128)}, ...) | async-done | bytes 20054032 | tf_op jit(solution)/shard_map/psum | solution.py:228
  860.9 4.0 fusion.53
  869.1 16.0 %all-reduce = (f32[768]{0:T(1024)S(1)}, f32[768]{0:T(1024)S(1)}) all-reduce(f32[768]{0:T(1024)S(1)} %get-tuple-element.181, f32[768]{0:T(1024)S(1)} %copy-done.54), channel_id=1, replica_groups=mesh['seq'=4,'dp'=8] {'dp'}, use_global_device_ids=true, to_apply=%region_16.17 | all-reduce | flops 1536 | bytes 12288 | tf_op jit(solution)/shard_map/psum | solution.py:228
  885.1 11.0 all-reduce.2
  896.2 3.3 add_bitcast_fusion
  899.4 328.8 %all-reduce.9.cloned.1.call-done = (f32[768,2304]{1,0:T(8,128)}, f32[768,768]{1,0:T(8,128)}, f32[768,2304]{1,0:T(8,128)}, f32[1152,768]{1,0:T(8,128)}) async-done(((f32[768,2304]{1,0:T(8,128)}, f32[768,768]{1,0:T(8,128)}, f32[768,2304]{1,0:T(8,128)}, f32[1152,768]{1,0:T(8,128)}), (f32[768,2304]{1,0:T(8,128)}, f32[768,768]{1,0:T(8,128)}, f32[768,2304]{1,0:T(8,128)}, ...) | async-done | bytes 20054032 | tf_op jit(solution)/shard_map/psum | solution.py:227
  1228.3 7.2 copy.122
  1236.9 3.6 copy.124
  (277 shorter events, 95.7 us)
Async XLA Ops:
  7.2 208.6 %copy-start = (bf16[768,2304]{1,0:T(8,128)(2,1)S(1)}, bf16[768,2304]{1,0:T(8,128)(2,1)}, u32[]{:S(2)}) copy-start(bf16[768,2304]{1,0:T(8,128)(2,1)} %param.20) | copy-start | bytes 10616836
  7.2 9.3 copy-start.52
  14.4 6.6 copy-start.44
  16.5 4.5 copy-start.46
  24.9 2.4 copy-start.35
  30.1 34.0 %all-to-all-start = ((bf16[512,3,4,192]{0,3,1,2:T(8,128)(2,1)}), bf16[512,3,4,192]{0,3,1,2:T(8,128)(2,1)}, u32[]{:S(2)}, u32[]{:S(2)}) async-start(bf16[512,3,4,192]{0,3,1,2:T(8,128)(2,1)} %pad_maximum_fusion), calls=%async_computation | async-start | bytes 4718592 | tf_op jit(solution)/shard_map/all_to_all | solution.py:158
  78.7 6.9 copy-start.3
  78.7 6.9 copy-start.23
  103.6 6.9 copy-start.3
  103.6 6.9 copy-start.23
  128.4 6.9 copy-start.3
  128.4 6.9 copy-start.23
  153.2 6.9 copy-start.3
  153.2 6.9 copy-start.23
  212.7 3.0 copy-start.25
  212.7 3.1 copy-start.38
  215.4 13.1 %copy-start.5 = (f32[512,768]{1,0:T(8,128)}, f32[512,768]{1,0:T(8,128)S(1)}, u32[]{:S(2)}) copy-start(f32[512,768]{1,0:T(8,128)S(1)} %get-tuple-element.278) | copy-start | bytes 4718596
  215.4 13.1 %copy-start.40 = (f32[512]{0:T(512)}, f32[512]{0:T(512)S(1)}, u32[]{:S(2)}) copy-start(f32[512]{0:T(512)S(1)} %broadcast_multiply_fusion) | copy-start | bytes 6148
  215.8 12.7 %copy-start.42 = (f32[512]{0:T(512)}, f32[512]{0:T(512)S(1)}, u32[]{:S(2)}) copy-start(f32[512]{0:T(512)S(1)} %fusion.65) | copy-start | bytes 6148
  225.7 2.8 copy-start.15
  229.2 2.7 copy-start.7
  233.0 13.4 %all-to-all-start.2 = ((bf16[512,4,192]{0,2,1:T(8,128)(2,1)}), bf16[512,4,192]{0,2,1:T(8,128)(2,1)}, u32[]{:S(2)}, u32[]{:S(2)}) async-start(bf16[512,4,192]{0,2,1:T(8,128)(2,1)} %bitcast.31), calls=%async_computation.2 | async-start | bytes 1572864 | tf_op jit(solution)/shard_map/all_to_all | solution.py:197
  262.4 4.6 copy-start.2
  270.5 10.7 slice-start
  274.9 6.3 slice-start.1
  274.9 6.3 copy-start.4
  274.9 6.3 copy-start.20
  293.8 4.6 copy-start.2
  301.8 10.7 slice-start
  306.2 6.3 slice-start.1
  306.2 6.3 copy-start.4
  306.3 6.3 copy-start.20
  325.1 4.6 copy-start.2
  333.2 10.7 slice-start
  337.6 6.3 slice-start.1
  337.6 6.3 copy-start.4
  337.6 6.3 copy-start.20
  356.5 4.6 copy-start.2
  364.6 10.7 slice-start
  369.0 6.3 slice-start.1
  369.0 6.3 copy-start.4
  369.0 6.3 copy-start.20
  387.9 5.1 copy-start.26
  387.9 5.1 copy-start.28
  387.9 50.7 %all-to-all-start.3 = ((bf16[2048,3,1,192]{3,1,2,0:T(4,128)(2,1)}), bf16[2048,3,1,192]{3,1,2,0:T(4,128)(2,1)}, u32[]{:S(2)}, u32[]{:S(2)}) async-start(bf16[2048,3,1,192]{3,1,2,0:T(4,128)(2,1)} %copy.80), calls=%async_computation.3 | async-start | bytes 8388608 | tf_op jit(solution)/shard_map/all_to_all | solution.py:209
  392.9 2.3 copy-start.12
  392.9 467.9 %all-reduce.7.cloned.1.call-start = ((), (), s32[]{:S(2)}) async-start(), calls=%async_computation.4 | async-start | bytes 40108032 | tf_op jit(solution)/shard_map/psum | solution.py:228
  393.0 2.2 copy-start.13
  395.2 3.0 copy-start.6
  395.2 3.0 copy-start.16
  395.2 3.0 copy-start.34
  395.2 2.9 copy-start.39
  395.2 2.9 copy-start.41
  395.2 2.9 copy-start.43
  464.5 763.7 %all-reduce.9.cloned.1.call-start = ((), (), s32[]{:S(2)}) async-start(), calls=%async_computation.5 | async-start | bytes 40108032 | tf_op jit(solution)/shard_map/psum | solution.py:227
  860.9 4.1 copy-start.17
  860.9 4.1 copy-start.31
  864.9 2.3 copy-start.51
  867.2 28.9 %copy-start.8 = (f32[512,768]{1,0:T(8,128)S(1)}, f32[512,768]{1,0:T(8,128)}, u32[]{:S(2)}) copy-start(f32[512,768]{1,0:T(8,128)} %copy-done.7) | copy-start | bytes 4718596
  867.2 28.9 %copy-start.49 = (f32[512]{0:T(512)S(1)}, f32[512]{0:T(512)}, u32[]{:S(2)}) copy-start(f32[512]{0:T(512)} %copy-done.48) | copy-start | bytes 6148
  1228.3 7.2 copy-start.29
  1228.3 8.6 copy-start.10
  1236.9 4.6 copy-start.18
  1236.9 6.4 copy-start.1
  (27 other events, 36.1 us)
Sparse Core Ops, SparseCore 0:
  464.7 396.1 all-reduce.6
  864.8 363.3 all-reduce.8
